TPU v7x, 32 devices: a whole 2x2x4 slice. The times are simulated.
32 devices in a mesh: rep: 4 (over y, x), fsdp: 4 (over z), tp: 2 (over core).
Axes of the slice: x: 2, y: 2, z: 4, core: 2. Of those that a mesh axis runs over, the one named last changes fastest.
Arguments:
- tokens: bfloat16 [4096, 8192], P(('rep', 'fsdp'), 'tp'), may hold values from -6 to 6
- cotangent: bfloat16 [4096, 512], P(('rep', 'fsdp'), 'tp'), may hold values from -6 to 6
- weight: bfloat16 [512, 8192], P('fsdp', 'tp'), may hold values from -0.0625 to 0.0625
- momentum: bfloat16 [4, 512, 8192], P('rep', 'fsdp', 'tp'), may hold values from -6 to 6
Outputs:
- projected: bfloat16 [4096, 512], P(('rep', 'fsdp'))
- update: float32 [512, 8192], P('fsdp', 'tp')
- momentum_out: float32 [4, 512, 8192], P('rep', 'fsdp', 'tp')
All inputs are finite; a program needn't handle non-finite values.
Results may differ from a plain program's by a relative error of at most 0.006.
Values may be sent and summed in bfloat16 or wider, within the bound.
A program may use at most 64 MiB of HBM per device.

v0:
```python
import math
import jax
import jax.numpy as jnp
from jax import lax
from jax.sharding import PartitionSpec as P

BETA_ONE = 0.9
BETA_TWO = 0.99
SOFT_WIDTH = 0.25


def soft_signs(gradient, moment):
    blended = BETA_ONE * moment + (1.0 - BETA_ONE) * gradient
    soft_sign = jnp.clip(blended / SOFT_WIDTH, -1.0, 1.0)
    renewed = BETA_TWO * moment + (1.0 - BETA_TWO) * gradient
    return (soft_sign, renewed)


def shards(tokens, cotangent, weight, momentum):
    cotangent_all = lax.all_gather(cotangent, "tp", axis=1, tiled=True)
    scale = 1.0 / math.sqrt(tokens.shape[0] * lax.axis_size("fsdp"))
    partial_out = lax.dot_general(
        tokens,
        lax.all_gather(weight, "fsdp", axis=0, tiled=True),
        (((1,), (1,)), ((), ())),
        preferred_element_type=jnp.float32,
    )
    projected = lax.psum(partial_out, "tp").astype(jnp.bfloat16)
    gradient = (
        lax.psum_scatter(
            lax.dot_general(
                cotangent_all, tokens, (((0,), (0,)), ((), ())), preferred_element_type=jnp.float32
            ).astype(jnp.bfloat16),
            "fsdp",
            scatter_dimension=0,
            tiled=True,
        ).astype(jnp.float32)
        * scale
    )
    soft_sign, renewed = soft_signs(gradient, momentum[0].astype(jnp.float32))
    received = lax.all_to_all(soft_sign[None], "rep", split_axis=2, concat_axis=0, tiled=True)
    share = jnp.clip(jnp.sum(received, axis=0), -1.0, 1.0)
    update = lax.all_gather(share, "rep", axis=1, tiled=True)
    update, renewed = (update, renewed[None])
    return (projected, update, renewed)


def solution(mesh):
    return jax.shard_map(
        shards,
        mesh=mesh,
        in_specs=(
            P(("rep", "fsdp"), "tp"),
            P(("rep", "fsdp"), "tp"),
            P("fsdp", "tp"),
            P("rep", "fsdp", "tp"),
        ),
        out_specs=(P(("rep", "fsdp"), None), P("fsdp", "tp"), P("rep", "fsdp", "tp")),
        check_vma=False,
    )
```

profile of v0, /device:TPU:0, one launch (start us, length us, event | category | flops | bytes accessed | tf_op | source)
XLA Modules:
  0.0 220.9 jit_solution(17796813475665733636)
XLA Ops:
  7.2 0.0 copy-start
  7.2 0.0 reduce-scatter.2.cloned.1.call-start
  7.2 2.5 %all_gather.10 = bf16[256,512]{1,0:T(8,128)(2,1)S(1)} all-gather(bf16[256,256]{1,0:T(8,128)(2,1)} %param.5), channel_id=1, replica_groups=mesh['rep'=4,'fsdp'=4,'tp'=2] {'tp'}, dimensions={1}, use_global_device_ids=true | all-gather | bytes 393216 | tf_op jit(solution)/shard_map/all_gather | solution.py:20
  9.7 0.0 copy-done
  9.7 3.3 %convolution_convert_fusion = bf16[512,4096]{1,0:T(8,128)(2,1)} fusion(bf16[256,512]{1,0:T(8,128)(2,1)S(1)} %all_gather.10, bf16[256,4096]{1,0:T(8,128)(2,1)S(1)} %copy-done), kind=kOutput, calls=%fused_computation | convolution fusion | flops 1075838976 | bytes 6553600 | tf_op jit(solution)/shard_map/dot_general | solution.py:31
  13.0 0.0 copy-start.1
  13.0 0.0 reduce-scatter.2.cloned.1.call-update
  13.0 0.0 all-gather.3.cloned.1.call-start
  13.0 0.7 all-gather.3.cloned.1.call-update
  13.7 0.0 all-gather.5.cloned.1.call-start
  13.8 78.8 %reduce-scatter.2.cloned.1.call-done = bf16[128,4096]{1,0:T(8,128)(2,1)} async-done(((bf16[512,4096]{1,0:T(8,128)(2,1)}), bf16[128,4096]{1,0:T(8,128)(2,1)}) %reduce-scatter.2.cloned.1.call-update) | async-done | bytes 1048592 | tf_op jit(solution)/shard_map/reduce_scatter | solution.py:30
  92.5 0.0 copy-done.1
  92.5 3.9 %fusion.7 = (f32[1,128,4096]{2,1,0:T(8,128)}, f32[1,128,4096]{2,1,0:T(8,128)}) fusion(bf16[1,128,4096]{2,1,0:T(8,128)(2,1)S(1)} %copy-done.1, bf16[128,4096]{1,0:T(8,128)(2,1)} %reduce-scatter.2.cloned.1.call-done), kind=kLoop, calls=%fused_computation.12 | loop fusion | flops 5242880 | bytes 6291456 | tf_op jit(solution)/shard_map/broadcast_in_dim | solution.py:44
  96.5 5.6 %copy.8 = f32[1,128,4096]{1,0,2:T(1,128)} copy(f32[1,128,4096]{2,1,0:T(8,128)} %get-tuple-element.7) | data formatting | bytes 4194304 | tf_op jit(solution)/shard_map/broadcast_in_dim | solution.py:41
  102.1 29.8 %all_to_all.12 = f32[1,128,4096]{1,0,2:T(1,128)} all-to-all(f32[1,128,4096]{1,0,2:T(1,128)} %copy.8), channel_id=1, replica_groups=mesh['rep'=4,'fsdp'=4,'tp'=2] {'rep'}, dimensions={2} | all-to-all | bytes 4194304 | tf_op jit(solution)/shard_map/all_to_all | solution.py:41
  131.9 1.8 reduce_sum.9
  133.7 0.8 broadcast_clamp_fusion
  134.5 0.0 all-gather.5.cloned.1.call-update
  134.5 40.9 %all-gather.3.cloned.1.call-done = bf16[512,4096]{1,0:T(8,128)(2,1)} async-done(((bf16[128,4096]{1,0:T(8,128)(2,1)}), bf16[512,4096]{1,0:T(8,128)(2,1)}) %all-gather.3.cloned.1.call-update) | async-done | bytes 4194320 | tf_op jit(solution)/shard_map/all_gather | solution.py:24
  175.4 3.5 %fusion.8 = f32[256,512]{1,0:T(8,128)S(1)} fusion(bf16[256,4096]{1,0:T(8,128)(2,1)S(1)} %copy-done, bf16[512,4096]{1,0:T(8,128)(2,1)} %all-gather.3.cloned.1.call-done), kind=kOutput, calls=%fused_computation.14 | convolution fusion | flops 1073741824 | bytes 6815744 | tf_op jit(solution)/shard_map/dot_general | solution.py:22
  178.8 5.3 %all-reduce.1 = bf16[256,512]{1,0:T(8,128)(2,1)} all-reduce(f32[256,512]{1,0:T(8,128)S(1)} %fusion.8), channel_id=1, replica_groups=mesh['rep'=4,'fsdp'=4,'tp'=2] {'tp'}, use_global_device_ids=true, to_apply=%region_0.0 | all-reduce | flops 131072 | bytes 786432 | tf_op jit(solution)/shard_map/psum | solution.py:28
  184.2 27.3 %all-gather.5.cloned.1.call-done = f32[128,4096]{0,1:T(8,128)} async-done(((f32[128,1024]{0,1:T(8,128)}), f32[128,4096]{0,1:T(8,128)}) %all-gather.5.cloned.1.call-update) | async-done | bytes 2097168 | tf_op jit(solution)/shard_map/all_gather | solution.py:43
  211.5 2.9 %copy.9 = f32[128,4096]{1,0:T(8,128)} copy(f32[128,4096]{0,1:T(8,128)} %all-gather.5.cloned.1.call-done) | data formatting | bytes 4194304
Async XLA Ops:
  7.2 2.5 %copy-start = (bf16[256,4096]{1,0:T(8,128)(2,1)S(1)}, bf16[256,4096]{1,0:T(8,128)(2,1)}, u32[]{:S(2)}) copy-start(bf16[256,4096]{1,0:T(8,128)(2,1)} %param.4) | copy-start | bytes 6291460
  7.2 85.4 %reduce-scatter.2.cloned.1.call-start = ((), (), s32[]{:S(2)}) async-start(), calls=%async_computation.3 | async-start | bytes 5242880 | tf_op jit(solution)/shard_map/reduce_scatter | solution.py:30
  13.0 79.6 %copy-start.1 = (bf16[1,128,4096]{2,1,0:T(8,128)(2,1)S(1)}, bf16[1,128,4096]{2,1,0:T(8,128)(2,1)}, u32[]{:S(2)}) copy-start(bf16[1,128,4096]{2,1,0:T(8,128)(2,1)} %param.7) | copy-start | bytes 3145732
  13.0 162.4 %all-gather.3.cloned.1.call-start = ((), (), s32[]{:S(2)}) async-start(), calls=%async_computation.2 | async-start | bytes 5242880 | tf_op jit(solution)/shard_map/all_gather | solution.py:24
  13.7 197.8 %all-gather.5.cloned.1.call-start = ((), (), s32[]{:S(2)}) async-start(), calls=%async_computation.4 | async-start | bytes 2621440 | tf_op jit(solution)/shard_map/all_gather | solution.py:43
Sparse Core Ops, SparseCore 0:
  13.1 79.3 reduce-scatter.1
  94.1 81.2 all-gather.2
  177.8 33.6 all-gather.4
where the time goes:
time: 221 us
  waiting for transfers between devices  148 us (67%)
  blocking collectives  37.6 us (17%)
  between operations  13.8 us (6%)
  local copies, waits for them, and re-layouts  8.53 us (4%)
  matrix products  6.73 us (3%)
  other arithmetic  6.52 us (3%)
    reduce_scatter x1, waiting for transfers between devices, shards(): lax.psum_scatter(lax.dot_general(cotangent_all, tokens, (((0,), (0,)), ((...  78.8 us
    all_gather x1, waiting for transfers between devices, shards(): lax.all_gather(weight, 'fsdp', axis=0, tiled=True)  40.9 us
    all_to_all x1, blocking collectives, shards(): lax.all_to_all(soft_sign[None], 'rep', split_axis=2, concat_axis=0, tiled...  29.8 us
    all_gather x1, waiting for transfers between devices, shards(): update = lax.all_gather(share, 'rep', axis=1, tiled=True)  27.3 us
    broadcast_in_dim x1, local copies, waits for them, and re-layouts, shards(): soft_sign[None]  5.64 us
    psum x1, blocking collectives, shards(): projected = lax.psum(partial_out, 'tp').astype(jnp.bfloat16)  5.32 us
  transfers between devices with their start and end apart: 3, of which 3 were waited for; matrix products, arithmetic and copies ran while one was open for 7% of the time, Pallas kernels for 0%

commit v1 on v0

--- a/solution.py
+++ b/solution.py
@@ -7,6 +7,22 @@
 BETA_ONE = 0.9
 BETA_TWO = 0.99
 SOFT_WIDTH = 0.25
+
+
+def gather_around(x, axis, dim):
+    ways, here, step = (lax.axis_size(axis), lax.axis_index(axis), x.shape[dim])
+    shape = [n * ways if d == dim else n for d, n in enumerate(x.shape)]
+    full = lax.dynamic_update_slice_in_dim(jnp.zeros(shape, x.dtype), x, here * step, axis=dim)
+    going_up = going_down = x
+    for far in range(1, ways // 2 + 1):
+        going_up = lax.ppermute(going_up, axis, [(d, (d + 1) % ways) for d in range(ways)])
+        full = lax.dynamic_update_slice_in_dim(full, going_up, (here - far) % ways * step, axis=dim)
+        if 2 * far < ways:
+            going_down = lax.ppermute(going_down, axis, [(d, (d - 1) % ways) for d in range(ways)])
+            full = lax.dynamic_update_slice_in_dim(
+                full, going_down, (here + far) % ways * step, axis=dim
+            )
+    return full
 
 
 def soft_signs(gradient, moment):
@@ -21,7 +37,7 @@
     scale = 1.0 / math.sqrt(tokens.shape[0] * lax.axis_size("fsdp"))
     partial_out = lax.dot_general(
         tokens,
-        lax.all_gather(weight, "fsdp", axis=0, tiled=True),
+        gather_around(weight, "fsdp", 0),
         (((1,), (1,)), ((), ())),
         preferred_element_type=jnp.float32,
     )

time: 221 us -> 205 us (0.928)
  blocking collectives: 37.6 us -> 7.29 us
  local copies, waits for them, and re-layouts: 8.53 us -> 20 us
  starting transfers between devices: 0.12 us -> 9.17 us
  waiting for transfers between devices: 148 us -> 141 us
    all_gather x1 -> x0, waiting for transfers between devices: 40.9 us -> none  [shards(): lax.all_gather(weight, 'fsdp', axis=0, tiled=True)]
    ppermute x0 -> x3, waiting for transfers between devices: none -> 38.1 us  [the longest x2 21.5 us: gather_around(): lax.ppermute(going_up, axis, [(d, (d + 1) % ways) for d in range(ways)])]
    all_to_all x1 -> x0, blocking collectives: 29.8 us -> none  [shards(): lax.all_to_all(soft_sign[None], 'rep', split_axis=2, concat_axis=0, tiled...]
    all_gather x1, waiting for transfers between devices: 27.3 us -> 0.01 us  [shards(): update = lax.all_gather(share, 'rep', axis=1, tiled=True)]
    all_to_all x0 -> x1, waiting for transfers between devices: none -> 23.3 us  [shards(): lax.all_to_all(soft_sign[None], 'rep', split_axis=2, concat_axis=0, tiled...]
    dynamic_update_slice x0 -> x4, local copies, waits for them, and re-layouts: none -> 8.18 us  [the longest x2 4.71 us: gather_around(): lax.dynamic_update_slice_in_dim(full, going_up, (here - far) % ways * ste...]
    ppermute x0 -> x3, starting transfers between devices: none -> 4.65 us  [the longest x1 3.1 us: gather_around(): lax.ppermute(going_down, axis, [(d, (d - 1) % ways) for d in range(ways)])]
    all_to_all x0 -> x1, starting transfers between devices: none -> 4.44 us  [shards(): lax.all_to_all(soft_sign[None], 'rep', split_axis=2, concat_axis=0, tiled...]
  transfers between devices with their start and end apart: 3 -> 6, of which waited for: 3 -> 4; matrix products, arithmetic and copies ran while one was open for 7% -> 9% of each run, Pallas kernels for 0% -> 0%
where the time goes in v1:
time: 205 us
  waiting for transfers between devices  141 us (69%)
  local copies, waits for them, and re-layouts  20 us (10%)
  between operations  14.1 us (7%)
  starting transfers between devices  9.17 us (4%)
  blocking collectives  7.29 us (4%)
  matrix products  6.68 us (3%)
  other arithmetic  6.51 us (3%)
    reduce_scatter x1, waiting for transfers between devices, shards(): lax.psum_scatter(lax.dot_general(cotangent_all, tokens, (((0,), (0,)), ((...  79.5 us
    all_to_all x1, waiting for transfers between devices, shards(): lax.all_to_all(soft_sign[None], 'rep', split_axis=2, concat_axis=0, tiled...  23.3 us
    ppermute x2, waiting for transfers between devices, gather_around(): lax.ppermute(going_up, axis, [(d, (d + 1) % ways) for d in range(ways)])  21.5 us
    ppermute x1, waiting for transfers between devices, gather_around(): lax.ppermute(going_down, axis, [(d, (d - 1) % ways) for d in range(ways)])  16.7 us
    broadcast_in_dim x1, local copies, waits for them, and re-layouts, shards(): soft_sign[None]  5.63 us
    psum x1, blocking collectives, shards(): projected = lax.psum(partial_out, 'tp').astype(jnp.bfloat16)  4.82 us
    dynamic_update_slice x2, local copies, waits for them, and re-layouts, gather_around(): lax.dynamic_update_slice_in_dim(full, going_up, (here - far) % ways * ste...  4.71 us
    all_to_all x1, starting transfers between devices, shards(): lax.all_to_all(soft_sign[None], 'rep', split_axis=2, concat_axis=0, tiled...  4.44 us
  transfers between devices with their start and end apart: 6, of which 4 were waited for; matrix products, arithmetic and copies ran while one was open for 9% of the time, Pallas kernels for 0%

profile of v1, /device:TPU:0, one launch (start us, length us, event | category | flops | bytes accessed | tf_op | source)
XLA Modules:
  0.0 204.8 jit_solution(9872126523283044738)
XLA Ops:
  7.2 0.0 copy-start
  7.2 0.0 reduce-scatter.2.cloned.1.call-start
  7.2 2.5 %all_gather.6 = bf16[256,512]{1,0:T(8,128)(2,1)S(1)} all-gather(bf16[256,256]{1,0:T(8,128)(2,1)} %param.5), channel_id=1, replica_groups=mesh['rep'=4,'fsdp'=4,'tp'=2] {'tp'}, dimensions={1}, use_global_device_ids=true | all-gather | bytes 393216 | tf_op jit(solution)/shard_map/all_gather | solution.py:36
  9.7 0.0 copy-done
  9.7 3.2 %convolution_convert_fusion = bf16[512,4096]{1,0:T(8,128)(2,1)} fusion(bf16[256,512]{1,0:T(8,128)(2,1)S(1)} %all_gather.6, bf16[256,4096]{1,0:T(8,128)(2,1)S(1)} %copy-done), kind=kOutput, calls=%fused_computation | convolution fusion | flops 1075838976 | bytes 6553600 | tf_op jit(solution)/shard_map/dot_general | solution.py:47
  12.9 0.0 copy-start.1
  12.9 0.0 reduce-scatter.2.cloned.1.call-update
  12.9 79.5 %reduce-scatter.2.cloned.1.call-done = bf16[128,4096]{1,0:T(8,128)(2,1)} async-done(((bf16[512,4096]{1,0:T(8,128)(2,1)}), bf16[128,4096]{1,0:T(8,128)(2,1)}) %reduce-scatter.2.cloned.1.call-update) | async-done | bytes 1048592 | tf_op jit(solution)/shard_map/reduce_scatter | solution.py:46
  92.5 0.0 copy-done.1
  92.5 3.9 %fusion.7 = (f32[1,128,4096]{2,1,0:T(8,128)}, f32[1,128,4096]{2,1,0:T(8,128)}) fusion(bf16[1,128,4096]{2,1,0:T(8,128)(2,1)S(1)} %copy-done.1, bf16[128,4096]{1,0:T(8,128)(2,1)} %reduce-scatter.2.cloned.1.call-done), kind=kLoop, calls=%fused_computation.12 | loop fusion | flops 5242880 | bytes 6291456 | tf_op jit(solution)/shard_map/broadcast_in_dim | solution.py:60
  96.4 5.6 %copy.10 = f32[1,128,4096]{1,0,2:T(1,128)} copy(f32[1,128,4096]{2,1,0:T(8,128)} %get-tuple-element.13) | data formatting | bytes 4194304 | tf_op jit(solution)/shard_map/broadcast_in_dim | solution.py:57
  102.0 4.4 %all-to-all-start = ((f32[1,128,4096]{1,0,2:T(1,128)}), f32[1,128,4096]{1,0,2:T(1,128)}, u32[]{:S(2)}, u32[]{:S(2)}) async-start(f32[1,128,4096]{1,0,2:T(1,128)} %copy.10), calls=%async_computation.1 | async-start | bytes 4194304 | tf_op jit(solution)/shard_map/all_to_all | solution.py:57
  106.5 0.0 all-gather.2.cloned.1.call-start
  106.5 1.6 collective-permute-start
  108.1 23.3 %all-to-all-done = f32[1,128,4096]{1,0,2:T(1,128)} async-done(((f32[1,128,4096]{1,0,2:T(1,128)}), f32[1,128,4096]{1,0,2:T(1,128)}, u32[]{:S(2)}, u32[]{:S(2)}) %all-to-all-start) | async-done | bytes 2097184 | tf_op jit(solution)/shard_map/all_to_all | solution.py:57
  131.4 1.8 reduce_sum.9
  133.2 0.8 broadcast_clamp_fusion
  134.0 0.0 all-gather.2.cloned.1.call-update
  134.0 3.1 %collective-permute-start.1 = (bf16[128,4096]{1,0:T(8,128)(2,1)}, bf16[128,4096]{1,0:T(8,128)(2,1)S(1)}, u32[]{:S(2)}, u32[]{:S(2)}) collective-permute-start(bf16[128,4096]{1,0:T(8,128)(2,1)} %param.6), channel_id=1, source_target_pairs={{0,6},{2,0},{4,2},{6,4},{1,7},{3,1},{5,3},{7,5},{8,14},{10,8},{12,... | collective-permute-start | bytes 3145736 | tf_op jit(solution)/shard_map/ppermute | solution.py:21
  137.1 0.0 collective-permute-done
  137.1 0.0 collective-permute-start.2
  137.1 2.4 %broadcast_in_dim.9 = bf16[512,4096]{1,0:T(8,128)(2,1)} broadcast(bf16[]{:T(256)} %constant.42.clone.1), dimensions={} | broadcast | bytes 4194306 | tf_op jit(solution)/shard_map/broadcast_in_dim | solution.py:15
  139.6 2.4 %constant_dynamic-update-slice_fusion.3 = bf16[512,4096]{1,0:T(8,128)(2,1)} fusion(bf16[512,4096]{1,0:T(8,128)(2,1)} %broadcast_in_dim.9, bf16[128,4096]{1,0:T(8,128)(2,1)} %param.6, s32[]{:T(128)S(6)} %select_n.27), kind=kLoop, calls=%fused_computation.18 | loop fusion | bytes 2097156 | tf_op jit(solution)/shard_map/dynamic_update_slice | solution.py:15
  141.9 2.4 %constant_dynamic-update-slice_fusion.2 = bf16[512,4096]{1,0:T(8,128)(2,1)} fusion(bf16[512,4096]{1,0:T(8,128)(2,1)} %constant_dynamic-update-slice_fusion.3, bf16[128,4096]{1,0:T(8,128)(2,1)} %collective-permute-done, s32[]{:T(128)S(6)} %select_n.29), kind=kLoop, calls=%fused_computation.17 | loop fusion | bytes 2097156 | tf_op jit(solution)/shard_map/dynamic_update_slice | solution.py:19
  144.3 16.7 %collective-permute-done.1 = bf16[128,4096]{1,0:T(8,128)(2,1)S(1)} collective-permute-done((bf16[128,4096]{1,0:T(8,128)(2,1)}, bf16[128,4096]{1,0:T(8,128)(2,1)S(1)}, u32[]{:S(2)}, u32[]{:S(2)}) %collective-permute-start.1) | collective-permute-done | bytes 1048608 | tf_op jit(solution)/shard_map/ppermute | solution.py:21
  161.0 1.1 constant_dynamic-update-slice_fusion.1
  162.1 21.5 %collective-permute-done.2 = bf16[128,4096]{1,0:T(8,128)(2,1)} collective-permute-done((bf16[128,4096]{1,0:T(8,128)(2,1)}, bf16[128,4096]{1,0:T(8,128)(2,1)}, u32[]{:S(2)}, u32[]{:S(2)}) %collective-permute-start.2) | collective-permute-done | bytes 1048608 | tf_op jit(solution)/shard_map/ppermute | solution.py:18
  183.6 2.3 %constant_dynamic-update-slice_fusion = bf16[512,4096]{1,0:T(8,128)(2,1)} fusion(bf16[512,4096]{1,0:T(8,128)(2,1)} %constant_dynamic-update-slice_fusion.1, bf16[128,4096]{1,0:T(8,128)(2,1)} %collective-permute-done.2, s32[]{:T(128)S(6)} %select_n.33), kind=kLoop, calls=%fused_computation.15 | loop fusion | bytes 2097156 | tf_op jit(solution)/shard_map/dynamic_update_slice | solution.py:19
  185.9 3.5 %convolution_bitcast_fusion = f32[256,512]{0,1:T(8,128)S(1)} fusion(bf16[512,4096]{1,0:T(8,128)(2,1)} %constant_dynamic-update-slice_fusion, bf16[256,4096]{1,0:T(8,128)(2,1)S(1)} %copy-done), kind=kOutput, calls=%fused_computation.13 | convolution fusion | flops 1073741824 | bytes 6815744 | tf_op jit(solution)/shard_map/dot_general | solution.py:38
  189.4 4.8 %all-reduce.1 = bf16[256,512]{0,1:T(8,128)(2,1)S(1)} all-reduce(f32[256,512]{0,1:T(8,128)S(1)} %convolution_bitcast_fusion), channel_id=1, replica_groups=mesh['rep'=4,'fsdp'=4,'tp'=2] {'tp'}, use_global_device_ids=true, to_apply=%region_0.1 | all-reduce | flops 131072 | bytes 786432 | tf_op jit(solution)/shard_map/psum | solution.py:44
  194.2 0.8 copy.11
  195.0 0.0 all-gather.2.cloned.1.call-done
  195.0 2.9 %copy.12 = f32[128,4096]{1,0:T(8,128)} copy(f32[128,4096]{0,1:T(8,128)} %all-gather.2.cloned.1.call-done) | data formatting | bytes 4194304
Async XLA Ops:
  7.2 2.5 %copy-start = (bf16[256,4096]{1,0:T(8,128)(2,1)S(1)}, bf16[256,4096]{1,0:T(8,128)(2,1)}, u32[]{:S(2)}) copy-start(bf16[256,4096]{1,0:T(8,128)(2,1)} %param.4) | copy-start | bytes 6291460
  7.2 85.3 %reduce-scatter.2.cloned.1.call-start = ((), (), s32[]{:S(2)}) async-start(), calls=%async_computation.2 | async-start | bytes 5242880 | tf_op jit(solution)/shard_map/reduce_scatter | solution.py:46
  12.9 79.6 %copy-start.1 = (bf16[1,128,4096]{2,1,0:T(8,128)(2,1)S(1)}, bf16[1,128,4096]{2,1,0:T(8,128)(2,1)}, u32[]{:S(2)}) copy-start(bf16[1,128,4096]{2,1,0:T(8,128)(2,1)} %param.7) | copy-start | bytes 3145732
  102.0 29.4 %all-to-all-start = ((f32[1,128,4096]{1,0,2:T(1,128)}), f32[1,128,4096]{1,0,2:T(1,128)}, u32[]{:S(2)}, u32[]{:S(2)}) async-start(f32[1,128,4096]{1,0,2:T(1,128)} %copy.10), calls=%async_computation.1 | async-start | bytes 4194304 | tf_op jit(solution)/shard_map/all_to_all | solution.py:57
  106.5 88.6 %all-gather.2.cloned.1.call-start = ((), (), s32[]{:S(2)}) async-start(), calls=%async_computation.3 | async-start | bytes 2621440 | tf_op jit(solution)/shard_map/all_gather | solution.py:59
  106.5 30.6 %collective-permute-start = (bf16[128,4096]{1,0:T(8,128)(2,1)}, bf16[128,4096]{1,0:T(8,128)(2,1)}, u32[]{:S(2)}, u32[]{:S(2)}) collective-permute-start(bf16[128,4096]{1,0:T(8,128)(2,1)} %param.6), channel_id=1, source_target_pairs={{0,2},{2,4},{4,6},{6,0},{1,3},{3,5},{5,7},{7,1},{8,10},{10,12},{12... | collective-permute-start | bytes 3145736 | tf_op jit(solution)/shard_map/ppermute | solution.py:18
  134.0 27.0 %collective-permute-start.1 = (bf16[128,4096]{1,0:T(8,128)(2,1)}, bf16[128,4096]{1,0:T(8,128)(2,1)S(1)}, u32[]{:S(2)}, u32[]{:S(2)}) collective-permute-start(bf16[128,4096]{1,0:T(8,128)(2,1)} %param.6), channel_id=1, source_target_pairs={{0,6},{2,0},{4,2},{6,4},{1,7},{3,1},{5,3},{7,5},{8,14},{10,8},{12,... | collective-permute-start | bytes 3145736 | tf_op jit(solution)/shard_map/ppermute | solution.py:21
  137.1 46.5 %collective-permute-start.2 = (bf16[128,4096]{1,0:T(8,128)(2,1)}, bf16[128,4096]{1,0:T(8,128)(2,1)}, u32[]{:S(2)}, u32[]{:S(2)}) collective-permute-start(bf16[128,4096]{1,0:T(8,128)(2,1)} %collective-permute-done), channel_id=1, source_target_pairs={{0,2},{2,4},{4,6},{6,0},{1,3},{3,5},{5,7},{7,1},{8,10},{10,12},{12... | collective-permute-start | bytes 3145736 | tf_op jit(solution)/shard_map/ppermute | solution.py:18
Sparse Core Ops, SparseCore 0:
  13.1 79.3 reduce-scatter.1
  134.1 34.9 all-gather.1
